TPU v7x, 32 devices: a whole 2x2x4 slice. The times are simulated.
32 devices in a mesh: snap: 4 (over z), cell: 8 (over y, x, core).
Axes of the slice: x: 2, y: 2, z: 4, core: 2. Of those that a mesh axis runs over, the one named last changes fastest.
Arguments:
- pressure: float32 [8320, 16384], P('snap', 'cell'), may hold values from -180 to 180
- block_starts: int32 [64], replicated, may hold values from 0 to 8064, as said below
- retained_bins: int32 [64], replicated, may hold values from 0 to 127
Outputs:
- spectral_gram: float32 [64, 2, 64, 64], P('snap')
Inputs may be any that keep to these rules, and one draw needn't show every extreme that they name: `block_starts`: the 64 values are distinct multiples of 128.
All inputs are finite; a program needn't handle non-finite values.
Results may differ from a plain program's by a relative error of at most 0.0003.
Values sent between devices are 32-bit elements; how exact they have to be, the bound alone decides.
A program may use at most 128 MiB of HBM per device.

v0:
```python
import functools

import jax
import jax.numpy as jnp
from jax import lax
from jax.experimental import pallas as pl
from jax.experimental.pallas import tpu as pltpu
from jax.sharding import PartitionSpec as P

NFFT = 256
LANES = 128
AHEAD = 3
MESH = pl.DeviceIdType.MESH


def make_table(bins):
    offsets = lax.broadcasted_iota(jnp.int32, (NFFT, bins.shape[1]), 0)
    window = 0.5 - 0.5 * jnp.cos(2.0 * jnp.pi * offsets.astype(jnp.float32) / NFFT)
    norm_factor = 1.0 / jnp.sqrt(jnp.sum(window * window, axis=0, keepdims=True))
    phase_steps = (bins * offsets) & (NFFT - 1)
    angles = 2.0 * jnp.pi * phase_steps.astype(jnp.float32) / NFFT
    return jnp.concatenate([window * norm_factor * jnp.cos(angles), -window * norm_factor * jnp.sin(angles)], 1)


def repeat(count, unroll, step):
    def body(turn, carry):
        for extra in range(unroll):
            step(turn * unroll + extra)
        return carry

    lax.fori_loop(0, count // unroll, body, 0)
    for rest in range(count // unroll * unroll, count):
        step(rest)


def pipeline_kernel(snap_count, cell_count, chunks, wide, kept_count, blocks, scale, pressure_ref, bins_ref, starts_ref, out_ref, held, half_held,
                    spectra, half_spectra, landed, grams, table_rows, table_parts, turns, sides, packed, cell_slots, own_cells, near_slots, lent_slots, far_sums, far_slot, own_part,
                    gathered, late_slots, own_sem, send_sem, recv_sem, half_own, half_send, half_recv, halo_send, halo_recv, keep_sem,
                    spec_send, spec_recv, cell_send, cell_recv, near_send, near_recv, lent_send, lent_recv, forward_send, forward_recv,
                    gather_send, gather_recv, late_send, late_recv, line_sem, flip_sem):
    my_snap, my_cell = lax.axis_index("snap"), lax.axis_index("cell")
    row_count = pressure_ref.shape[0]
    half_count = snap_count // 2
    my_half = my_snap // half_count
    half_start = my_half * half_count
    half_len = NFFT // 2
    half_rows = half_count * row_count
    half_blocks = blocks // 2
    halo = half_rows % half_len
    last = chunks - 1
    rows_out = 2 * kept_count
    groups = kept_count // snap_count // 2
    group_rows = 4 * half_blocks
    early_rows = groups * blocks // cell_count
    near = [half_start + lax.rem(my_snap + step, half_count) for step in range(1, half_count)]
    far = [half_count - my_half + step * (1 - 2 * my_half) for step in range(half_count)]
    others = near + far
    outer = my_half * (snap_count - 1)
    at_end = my_snap == outer

    def cell_peer(step):
        return lax.rem(my_cell + step, cell_count)

    bits = cell_count.bit_length() - 1

    def cell_flip(bit):
        return my_cell + 2 ** bit * (1 - 2 * lax.rem(my_cell // 2 ** bit, 2))

    def along(step):
        pl.when(my_snap > 0)(lambda: step(my_snap - 1, 1))
        pl.when(my_snap < snap_count - 1)(lambda: step(my_snap + 1, 0))

    barrier = pltpu.get_barrier_semaphore()
    along(lambda snap, side: pl.semaphore_signal(barrier, inc=1, device_id=(snap, my_cell), device_id_type=MESH))
    for bit in range(bits):
        pl.semaphore_signal(barrier, inc=1, device_id=(my_snap, cell_flip(bit)), device_id_type=MESH)
    pl.semaphore_wait(barrier, bits + jnp.minimum(my_snap, 1) + jnp.minimum(snap_count - 1 - my_snap, 1))

    def remote(source, target, send, recv, snap, cell):
        return pltpu.make_async_remote_copy(
            src_ref=source, dst_ref=target, send_sem=send, recv_sem=recv, device_id=(snap, cell), device_id_type=MESH
        )

    def columns(chunk, owner):
        return pl.ds(pl.multiple_of((chunk * snap_count + owner) * wide, wide), wide)

    def rows_of(source):
        return pl.ds(pl.multiple_of(source * row_count, 8), row_count)

    def sending(chunk, peer):
        return remote(pressure_ref.at[:, columns(chunk, peer)], held.at[chunk, rows_of(my_snap)],
                      send_sem.at[chunk, peer], recv_sem.at[chunk, my_snap], peer, my_cell)

    def arriving(chunk, peer):
        return remote(pressure_ref.at[:, columns(chunk, peer)], held.at[chunk, rows_of(peer)],
                      send_sem.at[chunk, peer], recv_sem.at[chunk, peer], peer, my_cell)

    def keeping(chunk):
        return pltpu.make_async_copy(pressure_ref.at[:, columns(chunk, my_snap)], held.at[chunk, rows_of(my_snap)], own_sem.at[chunk])

    def half_columns(peer, side):
        return columns(last, lax.rem(peer, half_count) + side * half_count)

    def half_place(source):
        return pl.ds(pl.multiple_of(my_half * halo + lax.rem(source, half_count) * row_count, 8), row_count)

    def half_sending(peer, side):
        return remote(pressure_ref.at[:, half_columns(peer, side)], half_held.at[side, half_place(my_snap)],
                      half_send.at[peer, side], half_recv.at[my_snap, side], peer, my_cell)

    def half_arriving(peer, side):
        return remote(pressure_ref.at[:, half_columns(my_snap, side)], half_held.at[side, half_place(peer)],
                      half_send.at[peer, side], half_recv.at[peer, side], peer, my_cell)

    def half_keeping(side):
        return pltpu.make_async_copy(pressure_ref.at[:, half_columns(my_snap, side)], half_held.at[side, half_place(my_snap)],
                                     half_own.at[side])

    def halo_sending(peer, side, half):
        first, place = (row_count - halo, 0) if half == 0 else (0, half_rows)
        return remote(pressure_ref.at[pl.ds(first, halo), half_columns(peer, side)], half_held.at[side, pl.ds(place, halo)],
                      halo_send.at[peer, side], halo_recv.at[side], peer, my_cell)

    def spectra_rows(owner, group):
        return pl.ds(pl.multiple_of((owner * groups + group) * group_rows, group_rows), group_rows)

    def spectra_sending(group, peer):
        return remote(half_spectra.at[:, spectra_rows(peer, group)], landed.at[my_snap, :, pl.ds(group * group_rows, group_rows)],
                      spec_send.at[group, peer], spec_recv.at[group, my_snap], peer, my_cell)

    def spectra_arriving(group, peer):
        return remote(half_spectra.at[:, spectra_rows(peer, group)], landed.at[peer, :, pl.ds(group * group_rows, group_rows)],
                      spec_send.at[group, peer], spec_recv.at[group, peer], peer, my_cell)

    def spectra_keeping():
        own = pl.ds(pl.multiple_of(my_snap * groups * group_rows, group_rows), groups * group_rows)
        return pltpu.make_async_copy(half_spectra.at[:, own], landed.at[my_snap], keep_sem.at[0])

    def at_middle(half, step):
        @pl.when(my_snap == half_count - 1 + half)
        def _():
            for peer in far:
                for side in range(2):
                    step(halo_sending(peer, side, half))

    at_cut = my_snap == half_count - 1 + my_half

    @pl.when(at_cut)
    def _():
        sending(0, far[0]).start()

    for turn in range(snap_count - 2):
        along(lambda snap, side, turn=turn: pl.semaphore_signal(
            line_sem.at[turn, side], inc=1, device_id=(snap, my_cell), device_id_type=MESH))
        along(lambda snap, side, turn=turn: pl.semaphore_wait(line_sem.at[turn, 1 - side], 1))
    for bit in range(bits):
        pl.semaphore_signal(flip_sem.at[bit], inc=1, device_id=(my_snap, cell_flip(bit)), device_id_type=MESH)
        pl.semaphore_wait(flip_sem.at[bit], 1)

    for half in range(2):
        at_middle(half, lambda copy: copy.start())
    for side in range(2):
        for peer in near:
            half_sending(peer, side).start()
        half_keeping(side).start()
    for chunk in range(last):
        for peer in near:
            sending(chunk, peer).start()
        keeping(chunk).start()
    def send_far(begun):
        for chunk in range(last):
            for peer in far[begun if chunk == 0 else 0:]:
                sending(chunk, peer).start()

    pl.when(at_cut)(lambda: send_far(1))

    table = make_table(bins_ref[...]).T
    for side in range(NFFT // LANES):
        for part in range(2):
            for slot in range(2 * snap_count):
                first = part * kept_count + slot * groups
                place = slot // 2 * 4 * groups + slot % 2 * 2 + part
                table_rows[side, pl.ds(place, groups, stride=4), :] = table[first:first + groups, side * LANES:(side + 1) * LANES]
    table = jnp.concatenate([table_rows[side] for side in range(NFFT // LANES)], 1)
    coarse = table.astype(jnp.bfloat16)
    table_parts[:rows_out] = coarse
    table_parts[rows_out:] = (table - coarse.astype(jnp.float32)).astype(jnp.bfloat16)

    lanes = 2 * blocks
    starts = jnp.concatenate([starts_ref[...]] * 2, 1).astype(jnp.float32)
    across = jnp.broadcast_to(starts, (lanes, lanes))
    down = across.T
    sides[0] = down
    sides[1] = across
    row = lax.broadcasted_iota(jnp.int32, (lanes, lanes), 0)
    lane = lax.broadcasted_iota(jnp.int32, (lanes, lanes), 1)
    same_side = (row < blocks) == (lane < blocks)
    row_slot = (half_len * jnp.where(row < blocks, row, row - blocks)).astype(jnp.float32)
    lane_slot = (half_len * jnp.where(lane < blocks, lane, lane - blocks)).astype(jnp.float32)
    turns[0] = jnp.where(same_side & (down == lane_slot), 1.0, 0.0).astype(jnp.bfloat16)
    turns[1] = jnp.where(same_side & (across == row_slot), 1.0, 0.0).astype(jnp.bfloat16)

    def split(data):
        coarse = data.astype(jnp.bfloat16)
        return coarse, (data - coarse.astype(jnp.float32)).astype(jnp.bfloat16)

    def thirds(data):
        coarse, rest = split(data)
        middle = data - coarse.astype(jnp.float32)
        return [coarse, rest, (middle - rest.astype(jnp.float32)).astype(jnp.bfloat16)]

    def reorder(tile):
        left = jnp.dot(turns[0, :blocks, :blocks], jnp.concatenate(thirds(tile), 1), preferred_element_type=jnp.float32)
        tile = (left[:, :lanes] + left[:, lanes:2 * lanes]) + left[:, 2 * lanes:]
        right = jnp.dot(jnp.concatenate(thirds(tile), 0), turns[1], preferred_element_type=jnp.float32)
        return (right[:blocks] + right[blocks:2 * blocks]) + right[2 * blocks:]

    def waves(windows):
        data_coarse, data_fine = split(jnp.concatenate(windows, 1))
        both = jnp.dot(table_parts[...], data_coarse, preferred_element_type=jnp.float32)
        rest = jnp.dot(table_parts[:rows_out], data_fine, preferred_element_type=jnp.float32)
        result = both[:rows_out] + (both[rows_out:] + rest)
        return [result[:, i * wide:(i + 1) * wide] for i in range(len(windows))]

    def window_rows(block):
        return pl.ds(pl.multiple_of(block * half_len, half_len), NFFT)

    def transform(chunk, first, count):
        def spread(block, width):
            results = waves([held[chunk, window_rows(block + i), :] for i in range(width)])
            for i, result in enumerate(results):
                spectra[pl.ds(block + i, rows_out, stride=blocks), :] = result

        repeat(count // 2, 2, lambda step: spread(first + 2 * step, 2))
        if count % 2:
            spread(first + count - 1, 1)

    def half_transform(block):
        results = waves([half_held[side, window_rows(block), :] for side in range(2)])
        for side, result in enumerate(results):
            half_spectra[side, pl.ds(block, rows_out, stride=half_blocks), :] = result

    for side in range(2):
        half_keeping(side).wait()
        for peer in near:
            half_arriving(peer, side).wait_recv()
        halo_sending(my_snap, side, 0).wait_recv()
    repeat(half_blocks, 2, half_transform)
    spectra_keeping().start()

    for peer in near:
        for group in range(groups):
            spectra_sending(group, peer).start()
    pl.when(jnp.logical_not(at_cut))(lambda: send_far(0))

    def send_spectra(group):
        for peer in reversed(far):
            spectra_sending(group, peer).start()

    for group in range(min(AHEAD, groups)):
        send_spectra(group)

    def gram_product(data):
        data_coarse, data_fine = split(data)
        right = jnp.concatenate([data_coarse, data_fine], 0)
        both = lax.dot_general(data_coarse, right, (((1,), (1,)), ((), ())), preferred_element_type=jnp.float32)
        cross = both[:, 2 * blocks:]
        return both[:, :2 * blocks] + (cross + cross.T)

    def chunk_product(place):
        return gram_product(spectra[pl.ds(pl.multiple_of(place * 2 * blocks, 2 * blocks), 2 * blocks), :])

    def complex_gram(whole):
        top, turned = whole[:blocks], pltpu.roll(whole[blocks:], blocks, 1)
        lane = lax.broadcasted_iota(jnp.int32, top.shape, 1)
        return jnp.where(lane < blocks, top + turned, top - turned)

    def pair_up(first, second):
        first, second = complex_gram(first), complex_gram(second)
        row = lax.broadcasted_iota(jnp.int32, first.shape, 0)
        lane = lax.broadcasted_iota(jnp.int32, first.shape, 1)
        left = jnp.where(row >= lane, first, pltpu.roll(first, blocks, 1))
        right = jnp.where(row >= lane - blocks, pltpu.roll(second, blocks, 1), second)
        return jnp.where(lane < blocks, left, right)

    high_start = -(-half_rows // half_len)
    low_count = (half_rows - NFFT) // half_len + 1
    for chunk in range(last):
        keeping(chunk).wait()
        for peer in near:
            arriving(chunk, peer).wait_recv()
        transform(chunk, my_half * high_start, low_count)
        for peer in far:
            arriving(chunk, peer).wait_recv()
        if chunk == last - 1:
            for group in range(AHEAD, min(2 * AHEAD, groups)):
                send_spectra(group)
        transform(chunk, low_count, high_start - low_count)
        transform(chunk, (1 - my_half) * high_start, low_count)
        if chunk < last - 1:
            def accumulate(place, chunk=chunk):
                grams[place] = chunk_product(place) if chunk == 0 else grams[place] + chunk_product(place)

            repeat(kept_count, 4, accumulate)

    def early_gram(place):
        return grams[place] + chunk_product(place) if last > 1 else chunk_product(place)

    def early_pack(pair):
        packed[pl.ds(pl.multiple_of(pair * blocks, blocks), blocks)] = pair_up(early_gram(2 * pair), early_gram(2 * pair + 1))

    def early_share(owner, cell):
        return pl.ds(pl.multiple_of(owner * groups * blocks + cell * early_rows, 8), early_rows)

    def scattering(owner, step):
        return remote(packed.at[early_share(owner, cell_peer(step))], cell_slots.at[step - 1, owner],
                      cell_send.at[step - 1, owner], cell_recv.at[step - 1, owner], my_snap, cell_peer(step))

    def near_exchanging(peer):
        return remote(own_cells.at[peer], near_slots.at[lax.rem(my_snap, half_count)], near_send.at[peer],
                      near_recv.at[lax.rem(my_snap, half_count)], peer, my_cell)

    def near_exchanged(peer):
        return remote(own_cells.at[peer], near_slots.at[lax.rem(peer, half_count)], near_send.at[peer],
                      near_recv.at[lax.rem(peer, half_count)], peer, my_cell)

    def lending(source):
        place = lax.rem(source, half_count)
        return remote(own_cells.at[pl.ds(half_count - half_start, half_count)], lent_slots.at[place], lent_send.at[0],
                      lent_recv.at[place], outer, my_cell)

    def forwarding(peer):
        return remote(far_sums.at[lax.rem(peer, half_count)], far_slot, forward_send.at[peer], forward_recv.at[0], peer, my_cell)

    def gather_rows(cell):
        return pl.ds(pl.multiple_of(cell * early_rows, 8), early_rows)

    def gathering(step):
        return remote(own_part, gathered.at[gather_rows(my_cell)], gather_send.at[step - 1], gather_recv.at[my_cell], my_snap, cell_peer(step))

    def gather_arriving(step):
        return remote(own_part, gathered.at[gather_rows(cell_peer(step))], gather_send.at[step - 1], gather_recv.at[cell_peer(step)],
                      my_snap, cell_peer(step))

    for owner in range(snap_count):
        repeat(groups, 2, lambda pair, owner=owner: early_pack(owner * groups + pair))
        for step in range(1, cell_count):
            scattering(owner, step).start()

    def early_exchange():
        for owner in range(snap_count):
            total = packed[early_share(owner, my_cell)]
            for step in range(1, cell_count):
                scattering(owner, step).wait_recv()
                total = total + cell_slots[step - 1, owner]
            own_cells[owner] = total
        for peer in near:
            near_exchanging(peer).start()
        pl.when(jnp.logical_not(at_end))(lambda: lending(my_snap).start())

    def early_forward():
        @pl.when(at_end)
        def _():
            total = own_cells[pl.ds(half_count - half_start, half_count)]
            for peer in near:
                lending(peer).wait_recv()
                total = total + lent_slots[lax.rem(peer, half_count)]
            far_sums[...] = total
            for peer in far:
                forwarding(peer).start()

    def early_gather():
        part = own_cells[my_snap]
        for peer in near:
            near_exchanged(peer).wait_recv()
            part = part + near_slots[lax.rem(peer, half_count)]
        forwarding(my_snap).wait_recv()
        part = part + far_slot[...]
        own_part[...] = part
        for step in range(1, cell_count):
            gathering(step).start()
        gathered[gather_rows(my_cell)] = part

    def early_collect():
        for step in range(1, cell_count):
            gather_arriving(step).wait_recv()

    def late_gram(group, member):
        sets = []
        for place in range(half_count):
            for side in range(2):
                rows = [
                    landed[half * half_count + place, side, pl.ds(group * group_rows + (2 * member + part) * half_blocks, half_blocks), :]
                    for part in range(2)
                    for half in range(2)
                ]
                sets.append(jnp.concatenate(rows, 0))
        return gram_product(jnp.concatenate(sets, 1))

    def late_sending(group, step):
        return remote(late_slots.at[group, my_cell], late_slots.at[group, my_cell], late_send.at[group, step - 1],
                      late_recv.at[group, my_cell], my_snap, cell_peer(step))

    def late_arriving(group, step):
        return remote(late_slots.at[group, my_cell], late_slots.at[group, cell_peer(step)], late_send.at[group, step - 1],
                      late_recv.at[group, cell_peer(step)], my_snap, cell_peer(step))

    def late_share(group):
        for peer in others:
            spectra_arriving(group, peer).wait_recv()
        if 2 * AHEAD <= group + AHEAD < groups:
            send_spectra(group + AHEAD)
        late_slots[group, my_cell] = pair_up(late_gram(group, 0), late_gram(group, 1))
        for step in range(1, cell_count):
            late_sending(group, step).start()

    def late_sum(group):
        for step in range(1, cell_count):
            late_arriving(group, step).wait_recv()
        total = late_slots[group, 0]
        for cell in range(1, cell_count):
            total = total + late_slots[group, cell]
        total = (total + gathered[pl.ds(group * blocks, blocks)]) * scale
        tile = reorder(total)
        turned = tile.T
        rolled = pltpu.roll(tile, blocks, 1)
        before, after = sides[0, :blocks, :blocks], sides[1, :blocks, :blocks]
        for member in range(2):
            straight = (tile if member == 0 else rolled)[:, :blocks]
            mirrored = turned[member * blocks:(member + 1) * blocks]
            place = member * groups + group
            out_ref[place, 0] = jnp.where(before >= after, straight, mirrored)
            out_ref[place, 1] = jnp.where(before == after, 0.0, jnp.where(before >= after, -mirrored, straight))

    spectra_keeping().wait()
    def finish_late(done):
        for group in done:
            for peer in far:
                spectra_sending(group, peer).wait_send()
            for step in range(1, cell_count):
                late_sending(group, step).wait_send()

    def finish_early():
        for half in range(2):
            at_middle(half, lambda copy: copy.wait_send())
        for peer in near:
            for side in range(2):
                half_sending(peer, side).wait_send()
            for group in range(groups):
                spectra_sending(group, peer).wait_send()
        for chunk in range(last):
            for peer in others:
                sending(chunk, peer).wait_send()
        for step in range(1, cell_count):
            gathering(step).wait_send()
            for owner in range(snap_count):
                scattering(owner, step).wait_send()
        for peer in near:
            near_exchanging(peer).wait_send()
        pl.when(jnp.logical_not(at_end))(lambda: lending(my_snap).wait_send())

        @pl.when(at_end)
        def _():
            for peer in far:
                forwarding(peer).wait_send()

    ended = max(groups - 2, 0)
    ready = min(5, groups - 1)
    steps = {}
    for turn, step in ((0, early_exchange), (1, early_forward), (3, early_gather), (ready, early_collect)):
        steps.setdefault(min(turn, groups - 1), []).append(step)
    for group in range(groups):
        late_share(group)
        for step in steps.get(group, []):
            step()
        if group >= ready:
            for done in range(0 if group == ready else group - 1, group):
                late_sum(done)
        if group == max(groups - 2, 0):
            finish_late(range(ended))
        if group == max(groups - 2, ready):
            finish_early()
    late_sum(groups - 1)

    finish_late(range(ended, groups))


def pipelined_grams(pressure, block_starts, retained_bins, snap_count, cell_count, blocks):
    row_count, width_local = pressure.shape
    wide = LANES
    chunks = width_local // snap_count // wide
    kept_count = retained_bins.shape[0]
    groups = kept_count // snap_count // 2
    early_rows = groups * blocks // cell_count
    lanes = 2 * blocks
    half_len = NFFT // 2
    half_rows = snap_count // 2 * row_count
    halo = half_rows % half_len
    assert cell_count & (cell_count - 1) == 0 and snap_count > 2
    assert halo == half_len // 2 and halo <= row_count and blocks % 2 == 0 and snap_count % 2 == 0
    whole_vmem = pl.BlockSpec(memory_space=pltpu.VMEM)
    scale = 1.0 / (width_local * cell_count)
    semaphores = pltpu.SemaphoreType.DMA
    return pl.pallas_call(
        functools.partial(pipeline_kernel, snap_count, cell_count, chunks, wide, kept_count, blocks, scale),
        out_shape=jax.ShapeDtypeStruct((2 * groups, 2, blocks, blocks), jnp.float32),
        in_specs=[pl.BlockSpec(memory_space=pl.ANY), whole_vmem, whole_vmem],
        out_specs=whole_vmem,
        scratch_shapes=[
            pltpu.VMEM((chunks - 1, snap_count * row_count, wide), jnp.float32),
            pltpu.VMEM((2, half_rows + halo, wide), jnp.float32),
            pltpu.VMEM((2 * kept_count * blocks, wide), jnp.float32),
            pltpu.VMEM((2, kept_count * blocks, wide), jnp.float32),
            pltpu.VMEM((snap_count, 2, 2 * groups * blocks, wide), jnp.float32),
            pltpu.VMEM((kept_count, lanes, lanes), jnp.float32),
            pltpu.VMEM((NFFT // LANES, 2 * kept_count, LANES), jnp.float32),
            pltpu.VMEM((4 * kept_count, NFFT), jnp.bfloat16),
            pltpu.VMEM((2, lanes, lanes), jnp.bfloat16),
            pltpu.VMEM((2, lanes, lanes), jnp.float32),
            pltpu.VMEM((snap_count * groups * blocks, lanes), jnp.float32),
            pltpu.VMEM((cell_count - 1, snap_count, early_rows, lanes), jnp.float32),
            pltpu.VMEM((snap_count, early_rows, lanes), jnp.float32),
            pltpu.VMEM((snap_count // 2, early_rows, lanes), jnp.float32),
            pltpu.VMEM((snap_count // 2, snap_count // 2, early_rows, lanes), jnp.float32),
            pltpu.VMEM((snap_count // 2, early_rows, lanes), jnp.float32),
            pltpu.VMEM((early_rows, lanes), jnp.float32),
            pltpu.VMEM((early_rows, lanes), jnp.float32),
            pltpu.VMEM((groups * blocks, lanes), jnp.float32),
            pltpu.VMEM((groups, cell_count, blocks, lanes), jnp.float32),
            semaphores((chunks,)),
            semaphores((chunks, snap_count)),
            semaphores((chunks, snap_count)),
            semaphores((2,)),
            semaphores((snap_count, 2)),
            semaphores((snap_count, 2)),
            semaphores((snap_count, 2)),
            semaphores((2,)),
            semaphores((1,)),
            semaphores((groups, snap_count)),
            semaphores((groups, snap_count)),
            semaphores((cell_count - 1, snap_count)),
            semaphores((cell_count - 1, snap_count)),
            semaphores((snap_count,)),
            semaphores((snap_count // 2,)),
            semaphores((1,)),
            semaphores((snap_count // 2,)),
            semaphores((snap_count,)),
            semaphores((1,)),
            semaphores((cell_count - 1,)),
            semaphores((cell_count,)),
            semaphores((groups, cell_count - 1)),
            semaphores((groups, cell_count)),
            pltpu.SemaphoreType.REGULAR((snap_count - 2, 2)),
            pltpu.SemaphoreType.REGULAR((cell_count.bit_length() - 1,)),
        ],
        compiler_params=pltpu.CompilerParams(collective_id=2, has_side_effects=True, vmem_limit_bytes=46 * 2**20),
    )(pressure, retained_bins.reshape(1, kept_count), block_starts.reshape(1, blocks))


def gather_kernel(snap_count, chunks, wide, kept_count, blocks, pressure_ref, bins_ref, out_ref, held, spectra, grams,
                  table_parts, own_sem, send_sem, recv_sem):
    my_snap, my_cell = lax.axis_index("snap"), lax.axis_index("cell")
    row_count = pressure_ref.shape[0]
    half_count = snap_count // 2
    my_half = my_snap // half_count
    half_len = NFFT // 2
    near = [my_half * half_count + lax.rem(my_snap + step, half_count) for step in range(1, half_count)]
    far = [(1 - my_half) * half_count + lax.rem(my_snap + step, half_count) for step in range(half_count)]

    barrier = pltpu.get_barrier_semaphore()
    for peer in near + far:
        pl.semaphore_signal(barrier, inc=1, device_id=(peer, my_cell), device_id_type=MESH)
    pl.semaphore_wait(barrier, snap_count - 1)

    def columns(chunk, owner):
        return pressure_ref.at[:, pl.ds(pl.multiple_of((chunk * snap_count + owner) * wide, wide), wide)]

    def landing(chunk, source):
        return held.at[chunk, pl.ds(pl.multiple_of(source * row_count, 8), row_count)]

    def sending(chunk, peer):
        return pltpu.make_async_remote_copy(
            src_ref=columns(chunk, peer),
            dst_ref=landing(chunk, my_snap),
            send_sem=send_sem.at[chunk, peer],
            recv_sem=recv_sem.at[chunk, my_snap],
            device_id=(peer, my_cell),
            device_id_type=MESH,
        )

    def arriving(chunk, peer):
        return pltpu.make_async_remote_copy(
            src_ref=columns(chunk, peer),
            dst_ref=landing(chunk, peer),
            send_sem=send_sem.at[chunk, peer],
            recv_sem=recv_sem.at[chunk, peer],
            device_id=(peer, my_cell),
            device_id_type=MESH,
        )

    def keeping(chunk):
        return pltpu.make_async_copy(columns(chunk, my_snap), landing(chunk, my_snap), own_sem.at[chunk])

    for chunk in range(chunks):
        for peer in near:
            sending(chunk, peer).start()
        keeping(chunk).start()
    for chunk in range(chunks):
        for peer in far:
            sending(chunk, peer).start()

    table = make_table(bins_ref[...]).T
    coarse = table.astype(jnp.bfloat16)
    rows_out = 2 * kept_count
    table_parts[:rows_out] = coarse
    table_parts[rows_out:] = (table - coarse.astype(jnp.float32)).astype(jnp.bfloat16)

    half_rows = snap_count * row_count // 2
    low_count = (half_rows - NFFT) // half_len + 1
    high_start = -(-half_rows // half_len)
    assert low_count == blocks - high_start

    def transform(chunk, first, count):
        def spread(block, width):
            data = jnp.concatenate(
                [held[chunk, pl.ds(pl.multiple_of((block + i) * half_len, half_len), NFFT), :] for i in range(width)], 1
            )
            data_coarse = data.astype(jnp.bfloat16)
            data_fine = (data - data_coarse.astype(jnp.float32)).astype(jnp.bfloat16)
            both = jnp.dot(table_parts[...], data_coarse, preferred_element_type=jnp.float32)
            rest = jnp.dot(table_parts[:rows_out], data_fine, preferred_element_type=jnp.float32)
            result = both[:rows_out] + (both[rows_out:] + rest)
            for i in range(width):
                spectra[pl.ds(block + i, rows_out, stride=blocks), :] = result[:, i * wide:(i + 1) * wide]

        repeat(count // 2, 2, lambda step: spread(first + 2 * step, 2))
        if count % 2:
            spread(first + count - 1, 1)

    def product(k):
        data = jnp.concatenate(
            [spectra[pl.ds(pl.multiple_of((k + part * kept_count) * blocks, blocks), blocks), :] for part in range(2)], 0
        )
        data_coarse = data.astype(jnp.bfloat16)
        data_fine = (data - data_coarse.astype(jnp.float32)).astype(jnp.bfloat16)
        right = jnp.concatenate([data_coarse, data_fine], 0)
        both = lax.dot_general(data_coarse, right, (((1,), (1,)), ((), ())), preferred_element_type=jnp.float32)
        cross = both[:, 2 * blocks:]
        return both[:, :2 * blocks] + (cross + cross.T)

    def complex_gram(k):
        whole = grams[k] + product(k) if chunks > 1 else product(k)
        top, turned = whole[:blocks], pltpu.roll(whole[blocks:], blocks, 1)
        lane = lax.broadcasted_iota(jnp.int32, top.shape, 1)
        return jnp.where(lane < blocks, top + turned, top - turned)

    for chunk in range(chunks):
        keeping(chunk).wait()
        for peer in near:
            arriving(chunk, peer).wait_recv()
        transform(chunk, my_half * high_start, low_count)
        for peer in far:
            arriving(chunk, peer).wait_recv()
        transform(chunk, low_count, high_start - low_count)
        transform(chunk, (1 - my_half) * high_start, low_count)
        if chunk < chunks - 1:
            def accumulate(k, chunk=chunk):
                grams[k] = product(k) if chunk == 0 else grams[k] + product(k)

            repeat(kept_count, 4, accumulate)

    pairs = kept_count // snap_count // 2

    def finish(place):
        k = place // pairs * (2 * pairs) + lax.rem(place, pairs)
        first, second = complex_gram(k), complex_gram(k + pairs)
        row = lax.broadcasted_iota(jnp.int32, first.shape, 0)
        lane = lax.broadcasted_iota(jnp.int32, first.shape, 1)
        left = jnp.where(row >= lane, first, pltpu.roll(first, blocks, 1))
        right = jnp.where(row >= lane - blocks, pltpu.roll(second, blocks, 1), second)
        return jnp.where(lane < blocks, left, right)

    def write(place):
        out_ref[place] = finish(place)

    repeat(kept_count // 2, 2, write)
    for chunk in range(chunks):
        for peer in near + far:
            sending(chunk, peer).wait_send()


def local_grams(pressure, retained_bins, snap_count, blocks):
    row_count, width_local = pressure.shape
    wide = LANES
    chunks = width_local // snap_count // wide
    kept_count = retained_bins.shape[0]
    whole_vmem = pl.BlockSpec(memory_space=pltpu.VMEM)
    return pl.pallas_call(
        functools.partial(gather_kernel, snap_count, chunks, wide, kept_count, blocks),
        out_shape=jax.ShapeDtypeStruct((kept_count // 2, blocks, 2 * blocks), jnp.float32),
        in_specs=[pl.BlockSpec(memory_space=pl.ANY), whole_vmem],
        out_specs=whole_vmem,
        scratch_shapes=[
            pltpu.VMEM((chunks, snap_count * row_count, wide), jnp.float32),
            pltpu.VMEM((2 * kept_count * blocks, wide), jnp.float32),
            pltpu.VMEM((kept_count, 2 * blocks, 2 * blocks), jnp.float32),
            pltpu.VMEM((4 * kept_count, NFFT), jnp.bfloat16),
            pltpu.SemaphoreType.DMA((chunks,)),
            pltpu.SemaphoreType.DMA((chunks, snap_count)),
            pltpu.SemaphoreType.DMA((chunks, snap_count)),
        ],
        compiler_params=pltpu.CompilerParams(collective_id=1, has_side_effects=True),
    )(pressure, retained_bins.reshape(1, kept_count))


def reduce_kernel(snap_count, cell_count, scale, gram_ref, out_ref, cell_slots, own_cells, snap_slots, own_part, gathered,
                  cell_send, cell_recv, snap_send, snap_recv, gather_send, gather_recv):
    my_snap, my_cell = lax.axis_index("snap"), lax.axis_index("cell")

    def cell_peer(step):
        return lax.rem(my_cell + step, cell_count)

    def snap_peer(step):
        return lax.rem(my_snap + step, snap_count)

    barrier = pltpu.get_barrier_semaphore()
    for step in range(1, cell_count):
        pl.semaphore_signal(barrier, inc=1, device_id=(my_snap, cell_peer(step)), device_id_type=MESH)
    for step in range(1, snap_count):
        pl.semaphore_signal(barrier, inc=1, device_id=(snap_peer(step), my_cell), device_id_type=MESH)
    pl.semaphore_wait(barrier, cell_count + snap_count - 2)

    scatters = [
        pltpu.make_async_remote_copy(
            src_ref=gram_ref.at[:, cell_peer(step)],
            dst_ref=cell_slots.at[step - 1],
            send_sem=cell_send.at[step - 1],
            recv_sem=cell_recv.at[step - 1],
            device_id=(my_snap, cell_peer(step)),
            device_id_type=MESH,
        )
        for step in range(1, cell_count)
    ]
    for copy in scatters:
        copy.start()
    total = gram_ref[:, my_cell]
    for step in range(1, cell_count):
        scatters[step - 1].wait_recv()
        total = total + cell_slots[step - 1]
    own_cells[...] = total

    exchanges = [
        pltpu.make_async_remote_copy(
            src_ref=own_cells.at[snap_peer(step)],
            dst_ref=snap_slots.at[step - 1],
            send_sem=snap_send.at[step - 1],
            recv_sem=snap_recv.at[step - 1],
            device_id=(snap_peer(step), my_cell),
            device_id_type=MESH,
        )
        for step in range(1, snap_count)
    ]
    for copy in exchanges:
        copy.start()
    part = own_cells[my_snap]
    for step in range(1, snap_count):
        exchanges[step - 1].wait_recv()
        part = part + snap_slots[step - 1]
    own_part[...] = part * scale

    gathers = [
        pltpu.make_async_remote_copy(
            src_ref=own_part,
            dst_ref=gathered.at[my_cell],
            send_sem=gather_send.at[step - 1],
            recv_sem=gather_recv.at[step - 1],
            device_id=(my_snap, cell_peer(step)),
            device_id_type=MESH,
        )
        for step in range(1, cell_count)
    ]
    for copy in gathers:
        copy.start()
    out_ref[my_cell] = own_part[...]
    for step in range(1, cell_count):
        gathers[step - 1].wait_recv()
        source = lax.rem(my_cell + cell_count - step, cell_count)
        out_ref[source] = gathered[source]
    for copy in scatters + exchanges + gathers:
        copy.wait_send()


def reduce_grams(packed, scale):
    snap_count, cell_count, rows, lanes = packed.shape
    whole_vmem = pl.BlockSpec(memory_space=pltpu.VMEM)
    return pl.pallas_call(
        functools.partial(reduce_kernel, snap_count, cell_count, scale),
        out_shape=jax.ShapeDtypeStruct((cell_count, rows, lanes), jnp.float32),
        in_specs=[whole_vmem],
        out_specs=whole_vmem,
        scratch_shapes=[
            pltpu.VMEM((cell_count - 1, snap_count, rows, lanes), jnp.float32),
            pltpu.VMEM((snap_count, rows, lanes), jnp.float32),
            pltpu.VMEM((snap_count - 1, rows, lanes), jnp.float32),
            pltpu.VMEM((rows, lanes), jnp.float32),
            pltpu.VMEM((cell_count, rows, lanes), jnp.float32),
            pltpu.SemaphoreType.DMA((cell_count - 1,)),
            pltpu.SemaphoreType.DMA((cell_count - 1,)),
            pltpu.SemaphoreType.DMA((snap_count - 1,)),
            pltpu.SemaphoreType.DMA((snap_count - 1,)),
            pltpu.SemaphoreType.DMA((cell_count - 1,)),
            pltpu.SemaphoreType.DMA((cell_count - 1,)),
        ],
        compiler_params=pltpu.CompilerParams(collective_id=0, has_side_effects=True),
    )(packed)


def on_device(pressure, block_starts, retained_bins):
    snap_count = lax.axis_size("snap")
    row_count, width_local = pressure.shape
    kept_count = retained_bins.shape[0]
    blocks = block_starts.shape[0]
    lower = jnp.arange(blocks)[:, None] >= jnp.arange(blocks)[None, :]
    cell_count = lax.axis_size("cell")
    pairs = kept_count // snap_count // 2
    if pairs * blocks % (8 * cell_count) == 0 and width_local // snap_count // LANES > 1:
        return pipelined_grams(pressure, block_starts, retained_bins, snap_count, cell_count, blocks)
    halves = local_grams(pressure, retained_bins, snap_count, blocks)
    packed = halves.reshape(snap_count, cell_count, pairs * blocks // cell_count, 2 * blocks)
    reduced = reduce_grams(packed, 1.0 / (width_local * cell_count))
    paired = reduced.reshape(pairs, blocks, 2 * blocks)
    joined = jnp.concatenate([paired[:, :, :blocks], paired[:, :, blocks:]], 0)
    mirrored = joined.transpose(0, 2, 1)
    diagonal = jnp.eye(blocks, dtype=bool)
    own_real = jnp.where(lower, joined, mirrored)
    own_imag = jnp.where(diagonal, 0.0, jnp.where(lower, -mirrored, joined))
    own_block = jnp.stack([own_real, own_imag], 1)
    order = (block_starts[:, None] // (NFFT // 2) == jnp.arange(blocks)[None, :]).astype(jnp.float32)
    turned = jnp.einsum("kpij,dj->kpid", own_block, order, precision=lax.Precision.HIGHEST)
    return jnp.einsum("bi,kpid->kpbd", order, turned, precision=lax.Precision.HIGHEST)


def solution(mesh):
    placed = (P("snap", "cell"), P(), P())
    return jax.shard_map(
        on_device,
        mesh=mesh,
        in_specs=placed,
        out_specs=P("snap", None, None, None),
        check_vma=False,
    )
```

profile of v0, /device:TPU:0, one launch (start us, length us, event | category | flops | bytes accessed | tf_op | source)
XLA Modules:
  0.0 383.4 jit_solution(16788334333977801915)
XLA Ops:
  0.0 0.0 copy-start
  0.0 0.7 copy-done
  0.7 0.0 copy-start.1
  0.7 0.7 copy-done.1
  1.3 381.1 %shard_map.37 = f32[16,2,64,64]{3,2,1,0:T(8,128)S(1)} custom-call(f32[2080,2048]{1,0:T(8,128)} %pressure_ref.1, s32[1,64]{1,0:T(1,128)S(1)} %bitcast.2, s32[1,64]{1,0:T(1,128)S(1)} %bitcast.3), custom_call_target="tpu_custom_call" | custom-call | tf_op jit(solution)/shard_map/pallas_call | solution.py:504
  382.5 1.0 copy.5
Async XLA Ops:
  0.0 0.7 copy-start
  0.7 0.7 copy-start.1
where the time goes:
time: 384 us; the launch traced here: 383 us
  Pallas kernels  381 us (99%)
    pallas_call x1, Pallas kernels, pipelined_grams(): pl.pallas_call(functools.partial(pipeline_kernel, snap_count, cell_count,...  381 us

commit v1 on v0

--- a/solution.py
+++ b/solution.py
@@ -33,7 +33,7 @@
         step(rest)
 
 
-def pipeline_kernel(snap_count, cell_count, chunks, wide, kept_count, blocks, scale, pressure_ref, bins_ref, starts_ref, out_ref, held, half_held,
+def pipeline_kernel(snap_count, cell_count, chunks, wide, kept_count, blocks, scale, pressure_ref, index_ref, out_ref, held, half_held,
                     spectra, half_spectra, landed, grams, table_rows, table_parts, turns, sides, packed, cell_slots, own_cells, near_slots, lent_slots, far_sums, far_slot, own_part,
                     gathered, late_slots, own_sem, send_sem, recv_sem, half_own, half_send, half_recv, halo_send, halo_recv, keep_sem,
                     spec_send, spec_recv, cell_send, cell_recv, near_send, near_recv, lent_send, lent_recv, forward_send, forward_recv,
@@ -174,7 +174,7 @@
 
     pl.when(at_cut)(lambda: send_far(1))
 
-    table = make_table(bins_ref[...]).T
+    table = make_table(index_ref[:1, :kept_count]).T
     for side in range(NFFT // LANES):
         for part in range(2):
             for slot in range(2 * snap_count):
@@ -187,7 +187,7 @@
     table_parts[rows_out:] = (table - coarse.astype(jnp.float32)).astype(jnp.bfloat16)
 
     lanes = 2 * blocks
-    starts = jnp.concatenate([starts_ref[...]] * 2, 1).astype(jnp.float32)
+    starts = jnp.concatenate([index_ref[1:, :blocks]] * 2, 1).astype(jnp.float32)
     across = jnp.broadcast_to(starts, (lanes, lanes))
     down = across.T
     sides[0] = down
@@ -496,7 +496,7 @@
     half_len = NFFT // 2
     half_rows = snap_count // 2 * row_count
     halo = half_rows % half_len
-    assert cell_count & (cell_count - 1) == 0 and snap_count > 2
+    assert kept_count == blocks and cell_count & (cell_count - 1) == 0 and snap_count > 2
     assert halo == half_len // 2 and halo <= row_count and blocks % 2 == 0 and snap_count % 2 == 0
     whole_vmem = pl.BlockSpec(memory_space=pltpu.VMEM)
     scale = 1.0 / (width_local * cell_count)
@@ -504,7 +504,7 @@
     return pl.pallas_call(
         functools.partial(pipeline_kernel, snap_count, cell_count, chunks, wide, kept_count, blocks, scale),
         out_shape=jax.ShapeDtypeStruct((2 * groups, 2, blocks, blocks), jnp.float32),
-        in_specs=[pl.BlockSpec(memory_space=pl.ANY), whole_vmem, whole_vmem],
+        in_specs=[pl.BlockSpec(memory_space=pl.ANY), whole_vmem],
         out_specs=whole_vmem,
         scratch_shapes=[
             pltpu.VMEM((chunks - 1, snap_count * row_count, wide), jnp.float32),
@@ -554,7 +554,7 @@
             pltpu.SemaphoreType.REGULAR((cell_count.bit_length() - 1,)),
         ],
         compiler_params=pltpu.CompilerParams(collective_id=2, has_side_effects=True, vmem_limit_bytes=46 * 2**20),
-    )(pressure, retained_bins.reshape(1, kept_count), block_starts.reshape(1, blocks))
+    )(pressure, jnp.stack([retained_bins, block_starts]))
 
 
 def gather_kernel(snap_count, chunks, wide, kept_count, blocks, pressure_ref, bins_ref, out_ref, held, spectra, grams,

time: 384 us -> 383 us (level)
  no operation moved by 1% of the time
where the time goes in v1:
time: 383 us
  Pallas kernels  381 us (99%)
    pallas_call x1, Pallas kernels, pipelined_grams(): pl.pallas_call(functools.partial(pipeline_kernel, snap_count, cell_count,...  381 us

profile of v1, /device:TPU:0, one launch (start us, length us, event | category | flops | bytes accessed | tf_op | source)
XLA Modules:
  0.0 382.8 jit_solution(15445168949812714106)
XLA Ops:
  0.0 0.7 pad_add_fusion.index_ref
  0.7 381.1 %shard_map.37 = f32[16,2,64,64]{3,2,1,0:T(8,128)S(1)} custom-call(f32[2080,2048]{1,0:T(8,128)} %pressure_ref.1, s32[2,64]{1,0:T(2,128)S(1)} %pad_add_fusion.index_ref), custom_call_target="tpu_custom_call" | custom-call | tf_op jit(solution)/shard_map/pallas_call | solution.py:504
  381.8 1.0 copy.5

commit v2 on v1

--- a/solution.py
+++ b/solution.py
@@ -260,10 +260,15 @@
     for group in range(min(AHEAD, groups)):
         send_spectra(group)
 
-    def gram_product(data):
+    def raw_product(data):
         data_coarse, data_fine = split(data)
         right = jnp.concatenate([data_coarse, data_fine], 0)
-        both = lax.dot_general(data_coarse, right, (((1,), (1,)), ((), ())), preferred_element_type=jnp.float32)
+        return lax.dot_general(data_coarse, right, (((1,), (1,)), ((), ())), preferred_element_type=jnp.float32)
+
+    def gram_product(data):
+        return symmetric(raw_product(data))
+
+    def symmetric(both):
         cross = both[:, 2 * blocks:]
         return both[:, :2 * blocks] + (cross + cross.T)
 
@@ -385,17 +390,16 @@
         for step in range(1, cell_count):
             gather_arriving(step).wait_recv()
 
-    def late_gram(group, member):
-        sets = []
-        for place in range(half_count):
-            for side in range(2):
-                rows = [
-                    landed[half * half_count + place, side, pl.ds(group * group_rows + (2 * member + part) * half_blocks, half_blocks), :]
-                    for part in range(2)
-                    for half in range(2)
-                ]
-                sets.append(jnp.concatenate(rows, 0))
-        return gram_product(jnp.concatenate(sets, 1))
+    def late_product(group, member, place):
+        sides = []
+        for side in range(2):
+            rows = [
+                landed[half * half_count + place, side, pl.ds(group * group_rows + (2 * member + part) * half_blocks, half_blocks), :]
+                for part in range(2)
+                for half in range(2)
+            ]
+            sides.append(jnp.concatenate(rows, 0))
+        return raw_product(jnp.concatenate(sides, 1))
 
     def late_sending(group, step):
         return remote(late_slots.at[group, my_cell], late_slots.at[group, my_cell], late_send.at[group, step - 1],
@@ -406,11 +410,16 @@
                       late_recv.at[group, cell_peer(step)], my_snap, cell_peer(step))
 
     def late_share(group):
-        for peer in others:
+        for peer in near:
             spectra_arriving(group, peer).wait_recv()
+        grams_here = [0.0, 0.0]
+        for peer in reversed(far):
+            spectra_arriving(group, peer).wait_recv()
+            for member in range(2):
+                grams_here[member] += late_product(group, member, lax.rem(peer, half_count))
         if 2 * AHEAD <= group + AHEAD < groups:
             send_spectra(group + AHEAD)
-        late_slots[group, my_cell] = pair_up(late_gram(group, 0), late_gram(group, 1))
+        late_slots[group, my_cell] = pair_up(symmetric(grams_here[0]), symmetric(grams_here[1]))
         for step in range(1, cell_count):
             late_sending(group, step).start()
 
@@ -480,9 +489,9 @@
             finish_late(range(ended))
         if group == max(groups - 2, ready):
             finish_early()
+    finish_late(range(ended, groups - 1))
     late_sum(groups - 1)
-
-    finish_late(range(ended, groups))
+    finish_late([groups - 1])
 
 
 def pipelined_grams(pressure, block_starts, retained_bins, snap_count, cell_count, blocks):

time: 383 us -> 383 us (level)
  no operation moved by 1% of the time
where the time goes in v2:
time: 383 us
  Pallas kernels  381 us (99%)
    pallas_call x1, Pallas kernels, pipelined_grams(): pl.pallas_call(functools.partial(pipeline_kernel, snap_count, cell_count,...  381 us

profile of v2, /device:TPU:0, one launch (start us, length us, event | category | flops | bytes accessed | tf_op | source)
XLA Modules:
  0.0 382.8 jit_solution(18186663124023018542)
XLA Ops:
  0.0 0.7 pad_add_fusion.index_ref
  0.7 381.1 %shard_map.37 = f32[16,2,64,64]{3,2,1,0:T(8,128)S(1)} custom-call(f32[2080,2048]{1,0:T(8,128)} %pressure_ref.1, s32[2,64]{1,0:T(2,128)S(1)} %pad_add_fusion.index_ref), custom_call_target="tpu_custom_call" | custom-call | tf_op jit(solution)/shard_map/pallas_call | solution.py:513
  381.8 1.0 copy.5

commit v3 on v2

--- a/solution.py
+++ b/solution.py
@@ -415,10 +415,10 @@
         grams_here = [0.0, 0.0]
         for peer in reversed(far):
             spectra_arriving(group, peer).wait_recv()
+            if peer is far[-1] and 2 * AHEAD <= group + AHEAD < groups:
+                send_spectra(group + AHEAD)
             for member in range(2):
                 grams_here[member] += late_product(group, member, lax.rem(peer, half_count))
-        if 2 * AHEAD <= group + AHEAD < groups:
-            send_spectra(group + AHEAD)
         late_slots[group, my_cell] = pair_up(symmetric(grams_here[0]), symmetric(grams_here[1]))
         for step in range(1, cell_count):
             late_sending(group, step).start()

time: 383 us -> 383 us (level)
  no operation moved by 1% of the time
where the time goes in v3:
time: 383 us
  Pallas kernels  381 us (99%)
    pallas_call x1, Pallas kernels, pipelined_grams(): pl.pallas_call(functools.partial(pipeline_kernel, snap_count, cell_count,...  381 us

profile of v3, /device:TPU:0, one launch (start us, length us, event | category | flops | bytes accessed | tf_op | source)
XLA Modules:
  0.0 382.8 jit_solution(2370920149147741049)
XLA Ops:
  0.0 0.7 pad_add_fusion.index_ref
  0.7 381.1 %shard_map.37 = f32[16,2,64,64]{3,2,1,0:T(8,128)S(1)} custom-call(f32[2080,2048]{1,0:T(8,128)} %pressure_ref.1, s32[2,64]{1,0:T(2,128)S(1)} %pad_add_fusion.index_ref), custom_call_target="tpu_custom_call" | custom-call | tf_op jit(solution)/shard_map/pallas_call | solution.py:513
  381.8 1.0 copy.5
